TPU v7x, 256 devices: a whole 4x4x8 slice. The times are simulated.
256 devices in a mesh: mp: 32 (over z, y_hi, core), dp: 8 (over x, y_lo).
Axes of the slice: x: 4, y: 4 (y_hi: 2, y_lo: 2; y = y_hi * 2 + y_lo), z: 8, core: 2. Of those that a mesh axis runs over, the one named last changes fastest.
Arguments:
- tokens: bfloat16 [1024, 8192], P('mp', 'dp'), may hold values from -6 to 6
- gate_weight: bfloat16 [8192, 16384], P('dp', 'mp'), may hold values from -0.0625 to 0.0625
- up_weight: bfloat16 [8192, 16384], P('dp', 'mp'), may hold values from -0.0625 to 0.0625
- down_weight: bfloat16 [16384, 8192], P('mp', 'dp'), may hold values from -0.046875 to 0.046875
- cotangent: bfloat16 [1024, 8192], P('mp', 'dp'), may hold values from -6 to 6
Outputs:
- mixed: bfloat16 [1024, 8192], P('mp', 'dp')
- token_grad: bfloat16 [1024, 8192], P('mp', 'dp')
- gate_grad: bfloat16 [8192, 16384], P('dp', 'mp')
- up_grad: bfloat16 [8192, 16384], P('dp', 'mp')
- down_grad: bfloat16 [16384, 8192], P('mp', 'dp')
All inputs are finite; a program needn't handle non-finite values.
Results may differ from a plain program's by a relative error of at most 0.005.
Values may be sent and summed in bfloat16 or wider, within the bound.
No kernel may reach another device: no remote copies, remote signals or barrier semaphores. Data moves between devices by JAX's collectives and lax.ppermute only.
A program may use at most 64 MiB of HBM per device.

v0:
```python
import jax
import jax.numpy as jnp
from jax import lax
from jax.sharding import PartitionSpec as P


def contract_rows(left, right):
    return lax.dot_general(
        left, right, (((0,), (0,)), ((), ())), preferred_element_type=jnp.float32
    )


def contract_cols(left, right):
    return lax.dot_general(
        left, right, (((1,), (1,)), ((), ())), preferred_element_type=jnp.float32
    )


def body(tokens, gate_weight, up_weight, down_weight, cotangent):
    token_all = lax.all_gather(tokens, "mp", axis=0, tiled=True)
    width = gate_weight.shape[1]
    block = token_all
    first = jnp.dot(block, gate_weight, preferred_element_type=jnp.float32)
    second = jnp.dot(block, up_weight, preferred_element_type=jnp.float32)
    both = lax.psum(jnp.concatenate([first, second], axis=1), "dp")
    gate = both[:, :width]
    up = both[:, width:]
    sig = jax.nn.sigmoid(gate)
    act = gate * sig
    hidden_part = (act * up).astype(jnp.bfloat16)
    block = hidden_part
    mixed = lax.psum_scatter(
        jnp.dot(block, down_weight, preferred_element_type=jnp.float32),
        "mp",
        scatter_dimension=0,
        tiled=True,
    ).astype(jnp.bfloat16)
    cot_all = lax.all_gather(cotangent, "mp", axis=0, tiled=True)
    down_grad = contract_rows(hidden_part, cot_all).astype(jnp.bfloat16)
    block = cot_all
    hidden_back = lax.psum(contract_cols(block, down_weight), "dp")
    pre_gate = (hidden_back * up * sig * (1.0 + gate * (1.0 - sig))).astype(jnp.bfloat16)
    pre_up = (hidden_back * act).astype(jnp.bfloat16)
    gate_all, up_all = (pre_gate, pre_up)
    gate_grad = contract_rows(token_all, gate_all).astype(jnp.bfloat16)
    up_grad = contract_rows(token_all, up_all).astype(jnp.bfloat16)
    first = gate_all
    second = up_all
    token_grad = lax.psum_scatter(
        contract_cols(first, gate_weight) + contract_cols(second, up_weight),
        "mp",
        scatter_dimension=0,
        tiled=True,
    ).astype(jnp.bfloat16)
    return (mixed, token_grad, gate_grad, up_grad, down_grad)


def solution(mesh):
    in_specs = (P("mp", "dp"), P("dp", "mp"), P("dp", "mp"), P("mp", "dp"), P("mp", "dp"))
    out_specs = (P("mp", "dp"), P("mp", "dp"), P("dp", "mp"), P("dp", "mp"), P("mp", "dp"))
    return jax.shard_map(body, mesh=mesh, in_specs=in_specs, out_specs=out_specs, check_vma=False)
```

profile of v0, /device:TPU:6, one launch (start us, length us, event | category | flops | bytes accessed | tf_op | source)
XLA Modules:
  0.0 717.8 jit_solution(3119205423730051404)
XLA Ops:
  7.2 0.0 copy-start
  7.2 0.0 all-gather.3.cloned.1.call-start
  7.2 0.7 all-gather.3.cloned.1.call-update
  7.9 0.0 all-gather.5.cloned.1.call-start
  8.0 0.7 all-gather.5.cloned.1.call-update
  8.7 0.0 all-reduce.3.cloned.1.call-start
  8.7 84.9 %all-gather.3.cloned.1.call-done = bf16[1024,1024]{1,0:T(8,128)(2,1)} async-done(((bf16[32,1024]{1,0:T(8,128)(2,1)}), bf16[1024,1024]{1,0:T(8,128)(2,1)}) %all-gather.3.cloned.1.call-update) | async-done | bytes 2097168 | tf_op jit(solution)/shard_map/all_gather | solution.py:20
  93.6 0.0 copy-start.4
  93.6 3.3 fusion.4
  96.9 0.0 copy-done
  96.9 0.0 copy-done.4
  96.9 1.3 fusion.3
  98.2 0.0 copy-start.3
  98.2 2.5 pad_maximum_fusion
  100.7 72.0 %all-gather.5.cloned.1.call-done = bf16[1024,1024]{1,0:T(8,128)(2,1)} async-done(((bf16[32,1024]{1,0:T(8,128)(2,1)}), bf16[1024,1024]{1,0:T(8,128)(2,1)}) %all-gather.5.cloned.1.call-update) | async-done | bytes 2097168 | tf_op jit(solution)/shard_map/all_gather | solution.py:38
  172.7 0.0 copy-done.3
  172.7 4.2 fusion.6
  176.9 0.0 all-reduce.3.cloned.1.call-update
  176.9 0.0 reduce-scatter.5.cloned.1.call-start
  177.0 262.9 %all-reduce.3.cloned.1.call-done = (f32[1024,1024]{0,1:T(8,128)}, f32[1024,512]{0,1:T(8,128)}) async-done(((f32[1024,1024]{0,1:T(8,128)}, f32[1024,512]{0,1:T(8,128)}), (f32[1024,1024]{0,1:T(8,128)}, f32[1024,512]{0,1:T(8,128)})) %all-reduce.3.cloned.1.call-update) | async-done | bytes 6291472 | tf_op jit(solution)/shard_map/psum | solution.py:25
  439.9 4.3 multiply_convert_fusion
  444.2 0.0 copy-start.2
  444.2 0.0 copy-start.1
  444.2 1.3 fusion.7
  445.5 0.0 copy-done.2
  445.5 0.3 copy-done.1
  445.8 3.3 convolution_add_fusion
  449.1 0.0 reduce-scatter.5.cloned.1.call-update
  449.1 0.2 reduce-scatter.3.cloned.1.call-start
  449.3 4.5 fusion.5
  453.8 0.0 reduce-scatter.3.cloned.1.call-update
  453.8 4.1 fusion.1
  458.0 2.3 copy.11
  460.3 3.8 fusion.2
  464.1 2.3 copy.12
  466.4 3.9 convolution_convert_fusion
  470.2 109.2 %reduce-scatter.5.cloned.1.call-done = f32[32,1024]{1,0:T(8,128)} async-done(((f32[1024,1024]{1,0:T(8,128)}), f32[32,1024]{1,0:T(8,128)}) %reduce-scatter.5.cloned.1.call-update) | async-done | bytes 131088 | tf_op jit(solution)/shard_map/reduce_scatter | solution.py:49
  579.4 1.5 convert_element_type.34
  581.0 128.8 %reduce-scatter.3.cloned.1.call-done = f32[32,1024]{1,0:T(8,128)} async-done(((f32[1024,1024]{1,0:T(8,128)}), f32[32,1024]{1,0:T(8,128)}) %reduce-scatter.3.cloned.1.call-update) | async-done | bytes 131088 | tf_op jit(solution)/shard_map/reduce_scatter | solution.py:32
  709.8 1.5 convert_element_type.31
Async XLA Ops:
  7.2 89.7 %copy-start = (bf16[1024,512]{1,0:T(8,128)(2,1)S(1)}, bf16[1024,512]{1,0:T(8,128)(2,1)}, u32[]{:S(2)}) copy-start(bf16[1024,512]{1,0:T(8,128)(2,1)} %param.6) | copy-start | bytes 3145732
  7.2 86.4 %all-gather.3.cloned.1.call-start = ((), (), s32[]{:S(2)}) async-start(), calls=%async_computation.2 | async-start | bytes 2162688 | tf_op jit(solution)/shard_map/all_gather | solution.py:20
  7.9 164.8 %all-gather.5.cloned.1.call-start = ((), (), s32[]{:S(2)}) async-start(), calls=%async_computation.4 | async-start | bytes 2162688 | tf_op jit(solution)/shard_map/all_gather | solution.py:38
  8.7 431.2 %all-reduce.3.cloned.1.call-start = ((), (), s32[]{:S(2)}) async-start(), calls=%async_computation.6 | async-start | bytes 12582912 | tf_op jit(solution)/shard_map/psum | solution.py:25
  93.6 3.3 copy-start.4
  98.2 74.5 %copy-start.3 = (bf16[512,1024]{1,0:T(8,128)(2,1)S(1)}, bf16[512,1024]{1,0:T(8,128)(2,1)}, u32[]{:S(2)}) copy-start(bf16[512,1024]{1,0:T(8,128)(2,1)} %param.8) | copy-start | bytes 3145732
  176.9 402.5 %reduce-scatter.5.cloned.1.call-start = ((), (), s32[]{:S(2)}) async-start(), calls=%async_computation.5 | async-start | bytes 4325376 | tf_op jit(solution)/shard_map/reduce_scatter | solution.py:49
  444.2 1.3 copy-start.2
  444.2 1.6 copy-start.1
  449.1 260.7 %reduce-scatter.3.cloned.1.call-start = ((), (), s32[]{:S(2)}) async-start(), calls=%async_computation.3 | async-start | bytes 4325376 | tf_op jit(solution)/shard_map/reduce_scatter | solution.py:32
Sparse Core Ops, SparseCore 0:
  10.8 82.7 all-gather.2
  96.4 76.3 all-gather.4
  177.1 262.8 all-reduce.2
  449.2 130.1 reduce-scatter.4
  583.5 126.2 reduce-scatter.2
where the time goes:
time: 718 us
  waiting for transfers between devices  659 us (92%)
  matrix products  29.7 us (4%)
  between operations  13.9 us (2%)
  other arithmetic  9.84 us (1%)
    psum x1, waiting for transfers between devices, body(): both = lax.psum(jnp.concatenate([first, second], axis=1), 'dp')  263 us
    reduce_scatter x1, waiting for transfers between devices, body(): lax.psum_scatter(jnp.dot(block, down_weight, preferred_element_type=jnp.f...  129 us
    reduce_scatter x1, waiting for transfers between devices, body(): lax.psum_scatter(contract_cols(first, gate_weight) + contract_cols(second...  109 us
    all_gather x1, waiting for transfers between devices, body(): token_all = lax.all_gather(tokens, 'mp', axis=0, tiled=True)  84.9 us
    all_gather x1, waiting for transfers between devices, body(): cot_all = lax.all_gather(cotangent, 'mp', axis=0, tiled=True)  72 us
  transfers between devices with their start and end apart: 5, of which 5 were waited for; matrix products, arithmetic and copies ran while one was open for 4% of the time, Pallas kernels for 0%

commit v1 on v0

--- a/solution.py
+++ b/solution.py
@@ -17,7 +17,10 @@
 
 
 def body(tokens, gate_weight, up_weight, down_weight, cotangent):
-    token_all = lax.all_gather(tokens, "mp", axis=0, tiled=True)
+    size = lax.axis_size("mp")
+    blocks = jnp.stack([tokens for _ in range(size)])
+    blocks = lax.all_to_all(blocks, "mp", split_axis=0, concat_axis=0)
+    token_all = jnp.concatenate(blocks, axis=0)
     width = gate_weight.shape[1]
     block = token_all
     first = jnp.dot(block, gate_weight, preferred_element_type=jnp.float32)

time: 718 us -> 658 us (0.916)
  waiting for transfers between devices: 659 us -> 585 us
  starting transfers between devices: 0.38 us -> 11.8 us
    all_gather x1 -> x0, waiting for transfers between devices: 84.9 us -> none  [body(): token_all = lax.all_gather(tokens, 'mp', axis=0, tiled=True)]
    all_to_all x0 -> x1, waiting for transfers between devices: none -> 52 us  [body(): blocks = lax.all_to_all(blocks, 'mp', split_axis=0, concat_axis=0)]
    all_gather x1, waiting for transfers between devices: 72 us -> 31.1 us  [body(): cot_all = lax.all_gather(cotangent, 'mp', axis=0, tiled=True)]
    all_to_all x0 -> x1, starting transfers between devices: none -> 11.5 us  [body(): blocks = lax.all_to_all(blocks, 'mp', split_axis=0, concat_axis=0)]
where the time goes in v1:
time: 658 us; the launch traced here: 657 us
  waiting for transfers between devices  585 us (89%)
  matrix products  29.7 us (5%)
  between operations  13.9 us (2%)
  starting transfers between devices  11.8 us (2%)
  other arithmetic  9.84 us (1%)
  local copies, waits for them, and re-layouts  7.38 us (1%)
    psum x1, waiting for transfers between devices, body(): both = lax.psum(jnp.concatenate([first, second], axis=1), 'dp')  263 us
    reduce_scatter x1, waiting for transfers between devices, body(): lax.psum_scatter(jnp.dot(block, down_weight, preferred_element_type=jnp.f...  129 us
    reduce_scatter x1, waiting for transfers between devices, body(): lax.psum_scatter(contract_cols(first, gate_weight) + contract_cols(second...  109 us
    all_to_all x1, waiting for transfers between devices, body(): blocks = lax.all_to_all(blocks, 'mp', split_axis=0, concat_axis=0)  52 us
    all_gather x1, waiting for transfers between devices, body(): cot_all = lax.all_gather(cotangent, 'mp', axis=0, tiled=True)  31.1 us
  transfers between devices with their start and end apart: 5, of which 5 were waited for; matrix products, arithmetic and copies ran while one was open for 4% of the time, Pallas kernels for 0%

profile of v1, /device:TPU:6, one launch (start us, length us, event | category | flops | bytes accessed | tf_op | source)
XLA Modules:
  0.0 657.3 jit_solution(4397207195503864926)
XLA Ops:
  7.2 0.0 copy-start
  7.2 2.5 stack.2
  9.7 11.5 %all-to-all-start = ((bf16[32,32,1024]{2,1,0:T(8,128)(2,1)}), bf16[32,32,1024]{2,1,0:T(8,128)(2,1)S(1)}, u32[]{:S(2)}, u32[]{:S(2)}) async-start(bf16[32,32,1024]{2,1,0:T(8,128)(2,1)} %stack.2), calls=%async_computation | async-start | bytes 4194304 | tf_op jit(solution)/shard_map/all_to_all | solution.py:22
  21.2 0.0 all-gather.2.cloned.1.call-start
  21.2 0.7 all-gather.2.cloned.1.call-update
  21.9 0.0 all-reduce.3.cloned.1.call-start
  22.0 52.0 %all-to-all-done = bf16[32,32,1024]{2,1,0:T(8,128)(2,1)S(1)} async-done(((bf16[32,32,1024]{2,1,0:T(8,128)(2,1)}), bf16[32,32,1024]{2,1,0:T(8,128)(2,1)S(1)}, u32[]{:S(2)}, u32[]{:S(2)}) %all-to-all-start) | async-done | bytes 2097184 | tf_op jit(solution)/shard_map/all_to_all | solution.py:22
  74.0 0.0 copy-start.1
  74.0 3.3 fusion.4
  77.3 0.0 copy-done.1
  77.3 0.0 copy-done
  77.3 1.3 fusion.3
  78.6 0.0 copy-start.4
  78.6 2.5 pad_maximum_fusion
  81.1 31.1 %all-gather.2.cloned.1.call-done = bf16[1024,1024]{1,0:T(8,128)(2,1)} async-done(((bf16[32,1024]{1,0:T(8,128)(2,1)}), bf16[1024,1024]{1,0:T(8,128)(2,1)}) %all-gather.2.cloned.1.call-update) | async-done | bytes 2097168 | tf_op jit(solution)/shard_map/all_gather | solution.py:41
  112.2 0.0 copy-done.4
  112.2 4.2 fusion.6
  116.4 0.0 all-reduce.3.cloned.1.call-update
  116.4 0.0 reduce-scatter.5.cloned.1.call-start
  116.4 262.9 %all-reduce.3.cloned.1.call-done = (f32[1024,1024]{0,1:T(8,128)}, f32[1024,512]{0,1:T(8,128)}) async-done(((f32[1024,1024]{0,1:T(8,128)}, f32[1024,512]{0,1:T(8,128)}), (f32[1024,1024]{0,1:T(8,128)}, f32[1024,512]{0,1:T(8,128)})) %all-reduce.3.cloned.1.call-update) | async-done | bytes 6291472 | tf_op jit(solution)/shard_map/psum | solution.py:28
  379.4 4.3 multiply_convert_fusion
  383.6 0.0 copy-start.3
  383.6 0.0 copy-start.2
  383.6 1.3 fusion.7
  385.0 0.0 copy-done.3
  385.0 0.3 copy-done.2
  385.2 3.3 convolution_add_fusion
  388.5 0.0 reduce-scatter.5.cloned.1.call-update
  388.6 0.2 reduce-scatter.3.cloned.1.call-start
  388.8 4.5 fusion.5
  393.3 0.0 reduce-scatter.3.cloned.1.call-update
  393.3 4.1 fusion.1
  397.4 2.3 copy.11
  399.7 3.8 fusion.2
  403.5 2.3 copy.12
  405.8 3.9 convolution_convert_fusion
  409.7 109.2 %reduce-scatter.5.cloned.1.call-done = f32[32,1024]{1,0:T(8,128)} async-done(((f32[1024,1024]{1,0:T(8,128)}), f32[32,1024]{1,0:T(8,128)}) %reduce-scatter.5.cloned.1.call-update) | async-done | bytes 131088 | tf_op jit(solution)/shard_map/reduce_scatter | solution.py:52
  518.9 1.5 convert_element_type.34
  520.4 128.8 %reduce-scatter.3.cloned.1.call-done = f32[32,1024]{1,0:T(8,128)} async-done(((f32[1024,1024]{1,0:T(8,128)}), f32[32,1024]{1,0:T(8,128)}) %reduce-scatter.3.cloned.1.call-update) | async-done | bytes 131088 | tf_op jit(solution)/shard_map/reduce_scatter | solution.py:35
  649.2 1.5 convert_element_type.31
Async XLA Ops:
  7.2 70.1 %copy-start = (bf16[1024,512]{1,0:T(8,128)(2,1)S(1)}, bf16[1024,512]{1,0:T(8,128)(2,1)}, u32[]{:S(2)}) copy-start(bf16[1024,512]{1,0:T(8,128)(2,1)} %param.6) | copy-start | bytes 3145732
  9.7 64.3 %all-to-all-start = ((bf16[32,32,1024]{2,1,0:T(8,128)(2,1)}), bf16[32,32,1024]{2,1,0:T(8,128)(2,1)S(1)}, u32[]{:S(2)}, u32[]{:S(2)}) async-start(bf16[32,32,1024]{2,1,0:T(8,128)(2,1)} %stack.2), calls=%async_computation | async-start | bytes 4194304 | tf_op jit(solution)/shard_map/all_to_all | solution.py:22
  21.2 91.0 %all-gather.2.cloned.1.call-start = ((), (), s32[]{:S(2)}) async-start(), calls=%async_computation.4 | async-start | bytes 2162688 | tf_op jit(solution)/shard_map/all_gather | solution.py:41
  21.9 357.4 %all-reduce.3.cloned.1.call-start = ((), (), s32[]{:S(2)}) async-start(), calls=%async_computation.6 | async-start | bytes 12582912 | tf_op jit(solution)/shard_map/psum | solution.py:28
  74.0 3.3 copy-start.1
  78.6 33.6 %copy-start.4 = (bf16[512,1024]{1,0:T(8,128)(2,1)S(1)}, bf16[512,1024]{1,0:T(8,128)(2,1)}, u32[]{:S(2)}) copy-start(bf16[512,1024]{1,0:T(8,128)(2,1)} %param.8) | copy-start | bytes 3145732
  116.4 402.5 %reduce-scatter.5.cloned.1.call-start = ((), (), s32[]{:S(2)}) async-start(), calls=%async_computation.5 | async-start | bytes 4325376 | tf_op jit(solution)/shard_map/reduce_scatter | solution.py:52
  383.6 1.3 copy-start.3
  383.6 1.6 copy-start.2
  388.6 260.6 %reduce-scatter.3.cloned.1.call-start = ((), (), s32[]{:S(2)}) async-start(), calls=%async_computation.3 | async-start | bytes 4325376 | tf_op jit(solution)/shard_map/reduce_scatter | solution.py:35
Sparse Core Ops, SparseCore 0:
  24.8 87.3 all-gather.1
  116.5 262.7 all-reduce.2
  388.7 130.1 reduce-scatter.4
  523.0 126.1 reduce-scatter.2
